TPU v7x, 32 devices: a whole 2x2x4 slice. The times are simulated.
32 devices in a mesh: groups: 2 (over y), tiles: 4 (over z), rhs: 2 (over x), sub: 2 (over core).
Axes of the slice: x: 2, y: 2, z: 4, core: 2. Of those that a mesh axis runs over, the one named last changes fastest.
Arguments:
- sources: bfloat16 [256, 8192], P('rhs', ('groups', 'tiles', 'sub')), parts along dimension 1, may hold values from -6 to 6
- basis_out: bfloat16 [384, 64, 512], P(('groups', 'tiles', 'rhs', 'sub')), parts along dimension 0, may hold values from -0.15625 to 0.15625
- basis_in: bfloat16 [384, 64, 512], P(('groups', 'tiles', 'rhs', 'sub')), parts along dimension 0, may hold values from -0.25 to 0.25
- tile_rank: int32 [384], P(('groups', 'tiles', 'rhs', 'sub')), parts along dimension 0, may hold values from 1 to 64, as said below
- tile_row: int32 [384], P(('groups', 'tiles', 'rhs', 'sub')), parts along dimension 0, may hold values from 0 to 7
- tile_col: int32 [384], P(('groups', 'tiles', 'rhs', 'sub')), parts along dimension 0, may hold values from 0 to 7
- near_blocks: bfloat16 [16, 16, 512, 512], P(('groups', 'tiles', 'sub')), parts along dimension 0, may hold values from -0.0625 to 0.0625
- near_col: int32 [16, 16], P(('groups', 'tiles', 'sub')), parts along dimension 0, may hold values from 0 to 7
- jacobi_inverse: bfloat16 [64, 128, 128], P(('groups', 'tiles', 'sub')), parts along dimension 0
Outputs:
- first_result: bfloat16 [256, 8192], P('rhs', ('groups', 'tiles', 'sub')), parts along dimension 1
- second_result: bfloat16 [256, 8192], P('rhs', ('groups', 'tiles', 'sub')), parts along dimension 1
There are 2 independent parts, one for each index of `groups`. A program takes and returns all parts, laid end to end along the dimension named above; each array names one. Nothing has to cross between parts.
Inputs may be any that keep to these rules, and one draw needn't show every extreme that they name: `tile_rank`: every rank lies in 1 to 64, and some tile has rank 64.
All inputs are finite; a program needn't handle non-finite values.
Results may differ from a plain program's by a relative error of at most 0.03.
Values may be sent and summed in bfloat16 or wider, within the bound.
No kernel may reach another device: no remote copies, remote signals or barrier semaphores. Data moves between devices by JAX's collectives and lax.ppermute only.
A program may use at most 128 MiB of HBM per device.

v0:
```python
import jax
import jax.numpy as jnp
from jax import lax
from jax.sharding import PartitionSpec as P

BLK = 512
RMAX = 64
JB = 128


def tile_terms(running, pieces, gathered):
    basis_out, basis_in, tile_rank, tile_row, tile_col = pieces
    picked = jnp.take(gathered, tile_col, axis=1)
    coefficients = jnp.einsum("ctq,trq->ctr", picked, basis_in, preferred_element_type=jnp.float32)
    rank_iota = lax.broadcasted_iota(jnp.int32, (1, tile_rank.shape[0], RMAX), 2)
    kept_mask = rank_iota < tile_rank[None, :, None]
    coefficients = jnp.where(kept_mask, coefficients, jnp.zeros_like(coefficients)).astype(
        jnp.bfloat16
    )
    contrib = jnp.einsum(
        "ctr,trp->ctp", coefficients, basis_out, preferred_element_type=jnp.float32
    )
    upper = contrib.astype(jnp.bfloat16)
    lower = (contrib - upper.astype(jnp.float32)).astype(jnp.bfloat16)
    block_iota = lax.broadcasted_iota(jnp.int32, (1, running.shape[1]), 1)
    onehot = (tile_row[:, None] == block_iota).astype(jnp.bfloat16)
    placed_upper = jnp.einsum("ctp,tb->cbp", upper, onehot, preferred_element_type=jnp.float32)
    placed_lower = jnp.einsum("ctp,tb->cbp", lower, onehot, preferred_element_type=jnp.float32)
    return placed_upper + placed_lower


def apply_operator(vector, tile_apply, near_blocks, near_col):
    columns = vector.shape[0]
    gathered = lax.all_gather(vector, ("tiles", "sub"), axis=1, tiled=True).reshape(
        columns, -1, BLK
    )
    zero_sums = jnp.zeros(gathered.shape, jnp.float32)
    far_field = tile_apply(zero_sums, gathered).reshape(columns, -1)
    far_field = lax.psum_scatter(
        far_field.astype(jnp.bfloat16), ("tiles", "sub"), scatter_dimension=1, tiled=True
    ).astype(jnp.float32)
    picked = jnp.take(gathered, near_col, axis=1)
    near_field = jnp.einsum(
        "cikq,ikpq->cip", picked, near_blocks, preferred_element_type=jnp.float32
    )
    return (far_field + near_field.reshape(columns, -1)).astype(jnp.bfloat16)


def precondition(field, jacobi_inverse):
    columns = field.shape[0]
    grouped = field.reshape(columns, -1, JB)
    result = jnp.einsum("cgq,gpq->cgp", grouped, jacobi_inverse, preferred_element_type=jnp.float32)
    return result.astype(jnp.bfloat16).reshape(columns, -1)


def local(
    sources,
    basis_out,
    basis_in,
    tile_rank,
    tile_row,
    tile_col,
    near_blocks,
    near_col,
    jacobi_inverse,
):

    def tile_apply(running, gathered):
        return tile_terms(
            running,
            (
                lax.all_gather(basis_out, "rhs", axis=0, tiled=True),
                lax.all_gather(basis_in, "rhs", axis=0, tiled=True),
                lax.all_gather(tile_rank, "rhs", axis=0, tiled=True),
                lax.all_gather(tile_row, "rhs", axis=0, tiled=True),
                lax.all_gather(tile_col, "rhs", axis=0, tiled=True),
            ),
            gathered,
        )

    first_result = precondition(
        apply_operator(sources, tile_apply, near_blocks, near_col), jacobi_inverse
    )
    second_result = precondition(
        apply_operator(first_result, tile_apply, near_blocks, near_col), jacobi_inverse
    )
    return (first_result, second_result)


def solution(mesh):
    return jax.shard_map(
        local,
        mesh=mesh,
        in_specs=(
            P("rhs", ("groups", "tiles", "sub")),
            P(("groups", "tiles", "rhs", "sub"), None, None),
            P(("groups", "tiles", "rhs", "sub"), None, None),
            P(("groups", "tiles", "rhs", "sub")),
            P(("groups", "tiles", "rhs", "sub")),
            P(("groups", "tiles", "rhs", "sub")),
            P(("groups", "tiles", "sub"), None, None, None),
            P(("groups", "tiles", "sub"), None),
            P(("groups", "tiles", "sub"), None, None),
        ),
        out_specs=(P("rhs", ("groups", "tiles", "sub")), P("rhs", ("groups", "tiles", "sub"))),
        check_vma=False,
    )
```

profile of v0, /device:TPU:0, one launch (start us, length us, event | category | flops | bytes accessed | tf_op | source)
XLA Modules:
  0.0 233.3 jit_solution(618950563438700425)
XLA Ops:
  7.2 1.7 copy.40
  9.0 0.7 all-gather.7.cloned.1.call-update
  9.7 0.7 all-gather.9.cloned.1.call-update
  10.5 1.2 dynamic-slice
  12.4 0.9 dynamic-update-slice
  13.2 0.8 dynamic-update-slice.1
  14.1 0.8 dynamic-update-slice.2
  14.9 5.2 %all-reduce.3 = (s32[24]{0:T(128)S(1)}, s32[24]{0:T(128)S(1)}, s32[24]{0:T(128)S(1)}) all-reduce(s32[24]{0:T(128)S(1)} %dynamic-update-slice.2, s32[24]{0:T(128)S(1)} %dynamic-update-slice.1, s32[24]{0:T(128)S(1)} %dynamic-update-slice), channel_id=1, replica_groups=mesh['groups'=2,'tiles'=4,'rhs'=2,'sub'=2] {'rhs'}, use_global_device_ids=true, to_apply=%add.2 | all-reduce | flops 72 | bytes 576
  20.2 14.8 %all-gather.5.cloned.1.call-done = bf16[128,4096]{0,1:T(8,128)(2,1)} async-done(((bf16[128,512]{0,1:T(8,128)(2,1)}), bf16[128,4096]{0,1:T(8,128)(2,1)}) %all-gather.5.cloned.1.call-update) | async-done | bytes 1048592 | tf_op jit(solution)/shard_map/all_gather | solution.py:34
  35.0 1.5 copy.41
  36.5 2.5 %gather_fusion = bf16[24,128,512]{2,1,0:T(8,128)(2,1)} fusion(bf16[128,8,512]{2,0,1:T(8,128)(2,1)S(1)} %copy.41, s32[1024]{0:T(1024)S(1)} %pad_clamp_fusion.1), kind=kCustom, calls=%fused_computation.clone | custom fusion | bytes 6291552 | tf_op jit(solution)/shard_map/jit(_take)/gather | solution.py:13
  39.0 24.4 %all-gather.7.cloned.1.call-done = bf16[24,64,512]{2,1,0:T(8,128)(2,1)} async-done(((bf16[12,64,512]{2,1,0:T(8,128)(2,1)}), bf16[24,64,512]{2,1,0:T(8,128)(2,1)}) %all-gather.7.cloned.1.call-update) | async-done | bytes 1572880 | tf_op jit(solution)/shard_map/all_gather | solution.py:73
  63.4 28.8 %all-gather.9.cloned.1.call-done = bf16[24,64,512]{2,1,0:T(8,128)(2,1)} async-done(((bf16[12,64,512]{2,1,0:T(8,128)(2,1)}), bf16[24,64,512]{2,1,0:T(8,128)(2,1)}) %all-gather.9.cloned.1.call-update) | async-done | bytes 1572880 | tf_op jit(solution)/shard_map/all_gather | solution.py:72
  92.2 7.7 %fusion.5 = (bf16[128,24,512]{2,0,1:T(8,128)(2,1)}, bf16[128,24,512]{2,0,1:T(8,128)(2,1)}) fusion(bf16[24,64,512]{2,1,0:T(8,128)(2,1)} %all-gather.9.cloned.1.call-done, bf16[24,64,512]{2,1,0:T(8,128)(2,1)} %all-gather.7.cloned.1.call-done, bf16[24,128,512]{2,1,0:T(8,128)(2,1)} %gather_fusion, pred[24]{0:T(512)(128)(4,1)S(1)} %compare_and_fusion, ...), kind=kOutput, calls=%fused_computation.13 | convolution fusion | flops 410910720 | bytes 12584472 | tf_op jit(solution)/shard_map/ctr,trp->ctp/dot_general | solution.py:20
  100.0 4.3 %fusion.14 = f32[8,128,512]{2,0,1:T(8,128)S(1)} fusion(bf16[128,24,512]{2,0,1:T(8,128)(2,1)} %get-tuple-element.17, s32[24]{0:T(128)S(1)} %get-tuple-element.14), kind=kOutput, calls=%fused_computation.22 | convolution fusion | flops 25166016 | bytes 5242976 | tf_op jit(solution)/shard_map/ctp,tb->cbp/dot_general | solution.py:28
  104.2 2.3 add_convert_fusion.1
  106.5 1.4 copy.56
  108.0 0.7 gather_fusion.1
  108.7 31.8 %reduce-scatter.3.cloned.1.call-done = bf16[128,512]{1,0:T(8,128)(2,1)} async-done(((bf16[128,4096]{1,0:T(8,128)(2,1)}), bf16[128,512]{1,0:T(8,128)(2,1)}) %reduce-scatter.3.cloned.1.call-update) | async-done | bytes 131088 | tf_op jit(solution)/shard_map/reduce_scatter | solution.py:39
  140.6 6.2 %fusion.93 = bf16[16,4,8,128]{3,2,1,0:T(8,128)(2,1)S(1)} fusion(bf16[1,16,512,512]{3,2,1,0:T(8,128)(2,1)} %param.19, bf16[16,128,512]{2,1,0:T(8,128)(2,1)S(1)} %gather_fusion.1, pred[16]{0:T(512)(128)(4,1)S(1)} %and_bitcast_fusion, bf16[128,512]{1,0:T(8,128)(2,1)} %reduce-scatter.3.cloned.1.call-done), kind=kOutput, calls=%fused_computation.57 | convolution fusion | flops 1074987008 | bytes 10747920 | tf_op jit(solution)/shard_map/cikq,ikpq->cip/dot_general | solution.py:43
  146.8 0.9 convolution_convert_fusion.1
  147.9 20.2 %all-gather.11.cloned.1.call-done = bf16[128,4096]{0,1:T(8,128)(2,1)} async-done(((bf16[128,512]{0,1:T(8,128)(2,1)}), bf16[128,4096]{0,1:T(8,128)(2,1)}) %all-gather.11.cloned.1.call-update) | async-done | bytes 1048592 | tf_op jit(solution)/shard_map/all_gather | solution.py:34
  168.1 3.9 %gather_fusion.2 = bf16[24,128,512]{1,2,0:T(8,128)(2,1)} fusion(bf16[128,8,512]{0,2,1:T(8,128)(2,1)} %bitcast.182, s32[1024]{0:T(1024)S(1)} %pad_clamp_fusion.1), kind=kCustom, calls=%fused_computation.2.clone | custom fusion | bytes 6291552 | tf_op jit(solution)/shard_map/jit(_take)/gather | solution.py:13
  172.0 6.7 %fusion.4 = (bf16[128,24,512]{2,0,1:T(8,128)(2,1)}, bf16[128,24,512]{2,0,1:T(8,128)(2,1)S(1)}) fusion(bf16[24,64,512]{2,1,0:T(8,128)(2,1)} %all-gather.9.cloned.1.call-done, bf16[24,64,512]{2,1,0:T(8,128)(2,1)} %all-gather.7.cloned.1.call-done, bf16[24,128,512]{1,2,0:T(8,128)(2,1)} %gather_fusion.2, pred[24]{0:T(512)(128)(4,1)S(1)} %compare_and_fusion, ...), kind=kOutput, calls=%fused_computation.10 | convolution fusion | flops 410910720 | bytes 12584472 | tf_op jit(solution)/shard_map/ctr,trp->ctp/dot_general | solution.py:20
  178.7 4.1 %fusion.10 = f32[8,128,512]{2,0,1:T(8,128)S(1)} fusion(bf16[128,24,512]{2,0,1:T(8,128)(2,1)} %get-tuple-element.15, s32[24]{0:T(128)S(1)} %get-tuple-element.14), kind=kOutput, calls=%fused_computation.18 | convolution fusion | flops 25166016 | bytes 5242976 | tf_op jit(solution)/shard_map/ctp,tb->cbp/dot_general | solution.py:28
  182.8 2.3 add_convert_fusion
  185.2 1.4 copy.57
  186.5 0.8 copy.51
  187.8 2.0 gather_fusion.3
  189.9 28.8 %reduce-scatter.5.cloned.1.call-done = bf16[128,512]{1,0:T(8,128)(2,1)} async-done(((bf16[128,4096]{1,0:T(8,128)(2,1)}), bf16[128,512]{1,0:T(8,128)(2,1)}) %reduce-scatter.5.cloned.1.call-update) | async-done | bytes 131088 | tf_op jit(solution)/shard_map/reduce_scatter | solution.py:39
  218.7 6.8 %fusion.88 = bf16[16,4,8,128]{3,2,1,0:T(8,128)(2,1)S(1)} fusion(bf16[1,16,512,512]{3,2,1,0:T(8,128)(2,1)} %param.19, bf16[16,128,512]{2,1,0:T(8,128)(2,1)} %gather_fusion.3, pred[16]{0:T(512)(128)(4,1)S(1)} %and_bitcast_fusion, bf16[128,512]{1,0:T(8,128)(2,1)} %reduce-scatter.5.cloned.1.call-done), kind=kOutput, calls=%fused_computation.56 | convolution fusion | flops 1074987008 | bytes 10747920 | tf_op jit(solution)/shard_map/cikq,ikpq->cip/dot_general | solution.py:43
  225.7 0.8 copy.52
  (32 shorter events, 1.4 us)
Async XLA Ops:
  7.2 139.6 %copy-start = (bf16[4,128,128]{2,1,0:T(8,128)(2,1)S(1)}, bf16[4,128,128]{2,1,0:T(8,128)(2,1)}, u32[]{:S(2)}) copy-start(bf16[4,128,128]{2,1,0:T(8,128)(2,1)} %param.21) | copy-start | bytes 393220
  7.2 27.8 %all-gather.5.cloned.1.call-start = ((), (), s32[]{:S(2)}) async-start(), calls=%async_computation.2 | async-start | bytes 1179648 | tf_op jit(solution)/shard_map/all_gather | solution.py:34
  8.9 54.5 %all-gather.7.cloned.1.call-start = ((), (), s32[]{:S(2)}) async-start(), calls=%async_computation.3 | async-start | bytes 2359296 | tf_op jit(solution)/shard_map/all_gather | solution.py:73
  9.7 82.5 %all-gather.9.cloned.1.call-start = ((), (), s32[]{:S(2)}) async-start(), calls=%async_computation.4 | async-start | bytes 2359296 | tf_op jit(solution)/shard_map/all_gather | solution.py:72
  10.4 130.1 %reduce-scatter.3.cloned.1.call-start = ((), (), s32[]{:S(2)}) async-start(), calls=%async_computation.5 | async-start | bytes 1179648 | tf_op jit(solution)/shard_map/reduce_scatter | solution.py:39
  100.0 4.3 %copy-start.2 = (bf16[128,24,512]{2,0,1:T(8,128)(2,1)S(1)}, bf16[128,24,512]{2,0,1:T(8,128)(2,1)}, u32[]{:S(2)}) copy-start(bf16[128,24,512]{2,0,1:T(8,128)(2,1)} %get-tuple-element.18) | copy-start | bytes 9437188
  106.5 1.5 copy-start.4
  107.9 60.2 %all-gather.11.cloned.1.call-start = ((), (), s32[]{:S(2)}) async-start(), calls=%async_computation.6 | async-start | bytes 1179648 | tf_op jit(solution)/shard_map/all_gather | solution.py:34
  147.7 71.0 %reduce-scatter.5.cloned.1.call-start = ((), (), s32[]{:S(2)}) async-start(), calls=%async_computation.7 | async-start | bytes 1179648 | tf_op jit(solution)/shard_map/reduce_scatter | solution.py:39
  185.1 1.4 copy-start.3
  185.1 2.2 copy-start.1
Sparse Core Ops, SparseCore 0:
  10.2 24.7 all-gather.4
  36.6 26.8 all-gather.6
  65.0 27.1 all-gather.8
  108.0 32.4 reduce-scatter.2
  147.8 20.2 all-gather.10
  186.7 31.9 reduce-scatter.4
where the time goes:
time: 234 us; the launch traced here: 233 us
  waiting for transfers between devices  150 us (64%)
  matrix products  41.5 us (18%)
  local copies, waits for them, and re-layouts  20.9 us (9%)
  between operations  14.9 us (6%)
  blocking collectives  5.19 us (2%)
    reduce_scatter x2, waiting for transfers between devices, apply_operator(): lax.psum_scatter(far_field.astype(jnp.bfloat16), ('tiles', 'sub'), scatte...  60.7 us
    all_gather x2, waiting for transfers between devices, apply_operator(): lax.all_gather(vector, ('tiles', 'sub'), axis=1, tiled=True)  35 us
    all_gather x1, waiting for transfers between devices, tile_apply(): lax.all_gather(basis_out, 'rhs', axis=0, tiled=True)  28.8 us
    all_gather x1, waiting for transfers between devices, tile_apply(): lax.all_gather(basis_in, 'rhs', axis=0, tiled=True)  24.4 us
    dot_general x2, matrix products, tile_terms(): jnp.einsum('ctr,trp->ctp', coefficients, basis_out, preferred_element_typ...  14.4 us
    dot_general x2, matrix products, apply_operator(): jnp.einsum('cikq,ikpq->cip', picked, near_blocks, preferred_element_type=...  13 us
    unnamed x22, local copies, waits for them, and re-layouts  9.77 us
    dot_general x2, matrix products, tile_terms(): jnp.einsum('ctp,tb->cbp', lower, onehot, preferred_element_type=jnp.float32)  8.39 us
  transfers between devices with their start and end apart: 6, of which 6 were waited for; matrix products, arithmetic and copies ran while one was open for 5% of the time, Pallas kernels for 0%

commit v1 on v0

--- a/solution.py
+++ b/solution.py
@@ -6,6 +6,22 @@
 BLK = 512
 RMAX = 64
 JB = 128
+
+
+def collect(x, axis, dim):
+    ways, here, step = (lax.axis_size(axis), lax.axis_index(axis), x.shape[dim])
+    dims = [n * ways if d == dim else n for d, n in enumerate(x.shape)]
+    full = lax.dynamic_update_slice_in_dim(jnp.zeros(dims, x.dtype), x, here * step, axis=dim)
+    going_up = going_down = x
+    for far in range(1, ways // 2 + 1):
+        going_up = lax.ppermute(going_up, axis, [(d, (d + 1) % ways) for d in range(ways)])
+        full = lax.dynamic_update_slice_in_dim(full, going_up, (here - far) % ways * step, axis=dim)
+        if 2 * far < ways:
+            going_down = lax.ppermute(going_down, axis, [(d, (d - 1) % ways) for d in range(ways)])
+            full = lax.dynamic_update_slice_in_dim(
+                full, going_down, (here + far) % ways * step, axis=dim
+            )
+    return full
 
 
 def tile_terms(running, pieces, gathered):
@@ -31,9 +47,7 @@
 
 def apply_operator(vector, tile_apply, near_blocks, near_col):
     columns = vector.shape[0]
-    gathered = lax.all_gather(vector, ("tiles", "sub"), axis=1, tiled=True).reshape(
-        columns, -1, BLK
-    )
+    gathered = collect(vector, ("tiles", "sub"), 1).reshape(columns, -1, BLK)
     zero_sums = jnp.zeros(gathered.shape, jnp.float32)
     far_field = tile_apply(zero_sums, gathered).reshape(columns, -1)
     far_field = lax.psum_scatter(

time: 234 us -> 211 us (0.902)
  waiting for transfers between devices: 150 us -> 111 us
  starting transfers between devices: 0.42 us -> 22.9 us
  local copies, waits for them, and re-layouts: 20.9 us -> 17.2 us
    all_gather x2 -> x0, waiting for transfers between devices: 35 us -> none  [apply_operator(): lax.all_gather(vector, ('tiles', 'sub'), axis=1, tiled=True)]
    ppermute x0 -> x14, waiting for transfers between devices: none -> 26.5 us  [the longest x8 26.3 us: collect(): lax.ppermute(going_up, axis, [(d, (d + 1) % ways) for d in range(ways)])]
    all_gather x1, waiting for transfers between devices: 24.4 us -> 0.01 us  [tile_apply(): lax.all_gather(basis_in, 'rhs', axis=0, tiled=True)]
    ppermute x0 -> x14, starting transfers between devices: none -> 22.7 us  [the longest x6 22.1 us: collect(): lax.ppermute(going_down, axis, [(d, (d - 1) % ways) for d in range(ways)])]
    all_gather x1, waiting for transfers between devices: 28.8 us -> 22.4 us  [tile_apply(): lax.all_gather(basis_out, 'rhs', axis=0, tiled=True)]
  transfers between devices with their start and end apart: 6 -> 18, of which waited for: 6 -> 11; matrix products, arithmetic and copies ran while one was open for 5% -> 5% of each run, Pallas kernels for 0% -> 0%
where the time goes in v1:
time: 211 us
  waiting for transfers between devices  111 us (53%)
  matrix products  41 us (19%)
  starting transfers between devices  22.9 us (11%)
  local copies, waits for them, and re-layouts  17.2 us (8%)
  between operations  14.9 us (7%)
  blocking collectives  4.25 us (2%)
    reduce_scatter x2, waiting for transfers between devices, apply_operator(): lax.psum_scatter(far_field.astype(jnp.bfloat16), ('tiles', 'sub'), scatte...  60.9 us
    ppermute x8, waiting for transfers between devices, collect(): lax.ppermute(going_up, axis, [(d, (d + 1) % ways) for d in range(ways)])  26.3 us
    all_gather x1, waiting for transfers between devices, tile_apply(): lax.all_gather(basis_out, 'rhs', axis=0, tiled=True)  22.4 us
    ppermute x6, starting transfers between devices, collect(): lax.ppermute(going_down, axis, [(d, (d - 1) % ways) for d in range(ways)])  22.1 us
    dot_general x2, matrix products, tile_terms(): jnp.einsum('ctr,trp->ctp', coefficients, basis_out, preferred_element_typ...  15 us
    dot_general x2, matrix products, apply_operator(): jnp.einsum('cikq,ikpq->cip', picked, near_blocks, preferred_element_type=...  12.4 us
    unnamed x22, local copies, waits for them, and re-layouts  9.16 us
    dot_general x2, matrix products, tile_terms(): jnp.einsum('ctp,tb->cbp', lower, onehot, preferred_element_type=jnp.float32)  8.54 us
  transfers between devices with their start and end apart: 18, of which 11 were waited for; matrix products, arithmetic and copies ran while one was open for 5% of the time, Pallas kernels for 0%

profile of v1, /device:TPU:0, one launch (start us, length us, event | category | flops | bytes accessed | tf_op | source)
XLA Modules:
  0.0 210.8 jit_solution(211242523118072559)
XLA Ops:
  8.0 1.0 copy.58
  9.5 4.1 %collective-permute-start.1 = (bf16[128,512]{0,1:T(8,128)(2,1)S(1)}, bf16[128,512]{0,1:T(8,128)(2,1)S(1)}, u32[]{:S(2)}, u32[]{:S(2)}) collective-permute-start(bf16[128,512]{0,1:T(8,128)(2,1)S(1)} %copy.58), channel_id=1, source_target_pairs={{0,13},{1,0},{4,1},{5,4},{8,5},{9,8},{12,9},{13,12},{2,15},{3,2},{... | collective-permute-start | bytes 393224 | tf_op jit(solution)/shard_map/ppermute | solution.py:20
  13.7 1.2 dynamic-slice
  15.6 0.9 dynamic-update-slice
  18.1 4.3 %all-reduce.3 = (s32[24]{0:T(128)S(1)}, s32[24]{0:T(128)S(1)}, s32[24]{0:T(128)S(1)}) all-reduce(s32[24]{0:T(128)S(1)} %dynamic-update-slice.2, s32[24]{0:T(128)S(1)} %dynamic-update-slice.1, s32[24]{0:T(128)S(1)} %dynamic-update-slice), channel_id=1, replica_groups=mesh['groups'=2,'tiles'=4,'rhs'=2,'sub'=2] {'rhs'}, use_global_device_ids=true, to_apply=%add.2 | all-reduce | flops 72 | bytes 576
  22.9 3.5 %collective-permute-start.3 = (bf16[128,512]{0,1:T(8,128)(2,1)S(1)}, bf16[128,512]{0,1:T(8,128)(2,1)S(1)}, u32[]{:S(2)}, u32[]{:S(2)}) collective-permute-start(bf16[128,512]{0,1:T(8,128)(2,1)S(1)} %collective-permute-done.1), channel_id=1, source_target_pairs={{0,13},{1,0},{4,1},{5,4},{8,5},{9,8},{12,9},{13,12},{2,15},{3,2},{... | collective-permute-start | bytes 393224 | tf_op jit(solution)/shard_map/ppermute | solution.py:20
  26.5 3.3 %collective-permute-done.2 = bf16[128,512]{0,1:T(8,128)(2,1)S(1)} collective-permute-done((bf16[128,512]{0,1:T(8,128)(2,1)S(1)}, bf16[128,512]{0,1:T(8,128)(2,1)S(1)}, u32[]{:S(2)}, u32[]{:S(2)}) %collective-permute-start.2) | collective-permute-done | bytes 131104 | tf_op jit(solution)/shard_map/ppermute | solution.py:17
  29.9 3.7 %collective-permute-start.5 = (bf16[128,512]{0,1:T(8,128)(2,1)S(1)}, bf16[128,512]{0,1:T(8,128)(2,1)S(1)}, u32[]{:S(2)}, u32[]{:S(2)}) collective-permute-start(bf16[128,512]{0,1:T(8,128)(2,1)S(1)} %collective-permute-done.3), channel_id=1, source_target_pairs={{0,13},{1,0},{4,1},{5,4},{8,5},{9,8},{12,9},{13,12},{2,15},{3,2},{... | collective-permute-start | bytes 393224 | tf_op jit(solution)/shard_map/ppermute | solution.py:20
  33.7 3.0 %collective-permute-done.4 = bf16[128,512]{0,1:T(8,128)(2,1)S(1)} collective-permute-done((bf16[128,512]{0,1:T(8,128)(2,1)S(1)}, bf16[128,512]{0,1:T(8,128)(2,1)S(1)}, u32[]{:S(2)}, u32[]{:S(2)}) %collective-permute-start.4) | collective-permute-done | bytes 131104 | tf_op jit(solution)/shard_map/ppermute | solution.py:17
  36.7 6.1 %collective-permute-done.6 = bf16[128,512]{0,1:T(8,128)(2,1)S(1)} collective-permute-done((bf16[128,512]{0,1:T(8,128)(2,1)S(1)}, bf16[128,512]{0,1:T(8,128)(2,1)S(1)}, u32[]{:S(2)}, u32[]{:S(2)}) %collective-permute-start.6) | collective-permute-done | bytes 131104 | tf_op jit(solution)/shard_map/ppermute | solution.py:17
  43.4 2.5 %gather_fusion = bf16[24,128,512]{2,1,0:T(8,128)(2,1)} fusion(bf16[128,8,512]{2,0,1:T(8,128)(2,1)S(1)} %copy.61, s32[1024]{0:T(1024)S(1)} %pad_clamp_fusion.1), kind=kCustom, calls=%fused_computation.clone | custom fusion | bytes 6291552 | tf_op jit(solution)/shard_map/jit(_take)/gather | solution.py:29
  45.9 22.4 %all-gather.5.cloned.1.call-done = bf16[24,64,512]{2,1,0:T(8,128)(2,1)} async-done(((bf16[12,64,512]{2,1,0:T(8,128)(2,1)}), bf16[24,64,512]{2,1,0:T(8,128)(2,1)}) %all-gather.5.cloned.1.call-update) | async-done | bytes 1572880 | tf_op jit(solution)/shard_map/all_gather | solution.py:86
  68.3 7.8 %fusion.5 = (bf16[128,24,512]{2,0,1:T(8,128)(2,1)}, bf16[128,24,512]{2,0,1:T(8,128)(2,1)}) fusion(bf16[24,64,512]{2,1,0:T(8,128)(2,1)} %all-gather.5.cloned.1.call-done, bf16[24,64,512]{2,1,0:T(8,128)(2,1)} %all-gather.3.cloned.1.call-done, bf16[24,128,512]{2,1,0:T(8,128)(2,1)} %gather_fusion, pred[24]{0:T(512)(128)(4,1)S(1)} %compare_and_fusion, ...), kind=kOutput, calls=%fused_computation.13 | convolution fusion | flops 410910720 | bytes 12584472 | tf_op jit(solution)/shard_map/ctr,trp->ctp/dot_general | solution.py:36
  76.0 4.3 %fusion.14 = f32[8,128,512]{2,0,1:T(8,128)S(1)} fusion(bf16[128,24,512]{2,0,1:T(8,128)(2,1)} %get-tuple-element.17, s32[24]{0:T(128)S(1)} %get-tuple-element.14), kind=kOutput, calls=%fused_computation.22 | convolution fusion | flops 25166016 | bytes 5242976 | tf_op jit(solution)/shard_map/ctp,tb->cbp/dot_general | solution.py:44
  80.3 2.3 %add_convert_fusion.1 = bf16[8,128,512]{2,0,1:T(8,128)(2,1)S(1)} fusion(f32[8,128,512]{2,0,1:T(8,128)S(1)} %fusion.14, bf16[128,24,512]{2,0,1:T(8,128)(2,1)S(1)} %copy-done.2, s32[24]{0:T(128)S(1)} %get-tuple-element.14), kind=kOutput, calls=%fused_computation.35 | convolution fusion | flops 26214592 | bytes 6291552 | tf_op jit(solution)/shard_map/ctp,tb->cbp/dot_general | solution.py:43
  82.6 1.4 copy.75
  84.8 31.9 %reduce-scatter.3.cloned.1.call-done = bf16[128,512]{1,0:T(8,128)(2,1)} async-done(((bf16[128,4096]{1,0:T(8,128)(2,1)}), bf16[128,512]{1,0:T(8,128)(2,1)}) %reduce-scatter.3.cloned.1.call-update) | async-done | bytes 131088 | tf_op jit(solution)/shard_map/reduce_scatter | solution.py:53
  116.7 6.2 %fusion.93 = bf16[16,4,8,128]{3,2,1,0:T(8,128)(2,1)S(1)} fusion(bf16[1,16,512,512]{3,2,1,0:T(8,128)(2,1)} %param.19, bf16[16,128,512]{2,1,0:T(8,128)(2,1)S(1)} %gather_fusion.1, pred[16]{0:T(512)(128)(4,1)S(1)} %and_bitcast_fusion, bf16[128,512]{1,0:T(8,128)(2,1)} %reduce-scatter.3.cloned.1.call-done), kind=kOutput, calls=%fused_computation.57 | convolution fusion | flops 1074987008 | bytes 10747920 | tf_op jit(solution)/shard_map/cikq,ikpq->cip/dot_general | solution.py:57
  123.2 3.5 %collective-permute-start.8 = (bf16[128,512]{0,1:T(8,128)(2,1)S(1)}, bf16[128,512]{0,1:T(8,128)(2,1)S(1)}, u32[]{:S(2)}, u32[]{:S(2)}) collective-permute-start(bf16[128,512]{0,1:T(8,128)(2,1)S(1)} %bitcast.189), channel_id=1, source_target_pairs={{0,13},{1,0},{4,1},{5,4},{8,5},{9,8},{12,9},{13,12},{2,15},{3,2},{... | collective-permute-start | bytes 393224 | tf_op jit(solution)/shard_map/ppermute | solution.py:20
  126.9 2.7 %collective-permute-done.7 = bf16[128,512]{0,1:T(8,128)(2,1)S(1)} collective-permute-done((bf16[128,512]{0,1:T(8,128)(2,1)S(1)}, bf16[128,512]{0,1:T(8,128)(2,1)S(1)}, u32[]{:S(2)}, u32[]{:S(2)}) %collective-permute-start.7) | collective-permute-done | bytes 131104 | tf_op jit(solution)/shard_map/ppermute | solution.py:17
  129.6 3.6 %collective-permute-start.10 = (bf16[128,512]{0,1:T(8,128)(2,1)S(1)}, bf16[128,512]{0,1:T(8,128)(2,1)S(1)}, u32[]{:S(2)}, u32[]{:S(2)}) collective-permute-start(bf16[128,512]{0,1:T(8,128)(2,1)S(1)} %collective-permute-done.8), channel_id=1, source_target_pairs={{0,13},{1,0},{4,1},{5,4},{8,5},{9,8},{12,9},{13,12},{2,15},{3,2},{... | collective-permute-start | bytes 393224 | tf_op jit(solution)/shard_map/ppermute | solution.py:20
  133.2 2.7 %collective-permute-done.9 = bf16[128,512]{0,1:T(8,128)(2,1)S(1)} collective-permute-done((bf16[128,512]{0,1:T(8,128)(2,1)S(1)}, bf16[128,512]{0,1:T(8,128)(2,1)S(1)}, u32[]{:S(2)}, u32[]{:S(2)}) %collective-permute-start.9) | collective-permute-done | bytes 131104 | tf_op jit(solution)/shard_map/ppermute | solution.py:17
  135.9 3.6 %collective-permute-start.12 = (bf16[128,512]{0,1:T(8,128)(2,1)S(1)}, bf16[128,512]{0,1:T(8,128)(2,1)S(1)}, u32[]{:S(2)}, u32[]{:S(2)}) collective-permute-start(bf16[128,512]{0,1:T(8,128)(2,1)S(1)} %collective-permute-done.10), channel_id=1, source_target_pairs={{0,13},{1,0},{4,1},{5,4},{8,5},{9,8},{12,9},{13,12},{2,15},{3,2},{... | collective-permute-start | bytes 393224 | tf_op jit(solution)/shard_map/ppermute | solution.py:20
  139.6 2.5 %collective-permute-done.11 = bf16[128,512]{0,1:T(8,128)(2,1)S(1)} collective-permute-done((bf16[128,512]{0,1:T(8,128)(2,1)S(1)}, bf16[128,512]{0,1:T(8,128)(2,1)S(1)}, u32[]{:S(2)}, u32[]{:S(2)}) %collective-permute-start.11) | collective-permute-done | bytes 131104 | tf_op jit(solution)/shard_map/ppermute | solution.py:17
  142.1 6.1 %collective-permute-done.13 = bf16[128,512]{0,1:T(8,128)(2,1)S(1)} collective-permute-done((bf16[128,512]{0,1:T(8,128)(2,1)S(1)}, bf16[128,512]{0,1:T(8,128)(2,1)S(1)}, u32[]{:S(2)}, u32[]{:S(2)}) %collective-permute-start.13) | collective-permute-done | bytes 131104 | tf_op jit(solution)/shard_map/ppermute | solution.py:17
  148.8 2.5 %gather_fusion.2 = bf16[24,128,512]{2,1,0:T(8,128)(2,1)} fusion(bf16[128,8,512]{2,0,1:T(8,128)(2,1)S(1)} %copy.66, s32[1024]{0:T(1024)S(1)} %pad_clamp_fusion.1), kind=kCustom, calls=%fused_computation.2.clone | custom fusion | bytes 6291552 | tf_op jit(solution)/shard_map/jit(_take)/gather | solution.py:29
  151.3 7.3 %fusion.4 = (bf16[128,24,512]{2,0,1:T(8,128)(2,1)}, bf16[128,24,512]{2,0,1:T(8,128)(2,1)}) fusion(bf16[24,64,512]{2,1,0:T(8,128)(2,1)} %all-gather.5.cloned.1.call-done, bf16[24,64,512]{2,1,0:T(8,128)(2,1)S(1)} %copy-done.3, bf16[24,128,512]{2,1,0:T(8,128)(2,1)} %gather_fusion.2, pred[24]{0:T(512)(128)(4,1)S(1)} %compare_and_fusion, ...), kind=kOutput, calls=%fused_computation.10 | convolution fusion | flops 410910720 | bytes 12584472 | tf_op jit(solution)/shard_map/ctr,trp->ctp/dot_general | solution.py:36
  158.6 4.3 %fusion.10 = f32[8,128,512]{2,0,1:T(8,128)S(1)} fusion(bf16[128,24,512]{2,0,1:T(8,128)(2,1)} %get-tuple-element.15, s32[24]{0:T(128)S(1)} %get-tuple-element.14), kind=kOutput, calls=%fused_computation.18 | convolution fusion | flops 25166016 | bytes 5242976 | tf_op jit(solution)/shard_map/ctp,tb->cbp/dot_general | solution.py:44
  162.8 2.3 %add_convert_fusion = bf16[8,128,512]{2,0,1:T(8,128)(2,1)S(1)} fusion(f32[8,128,512]{2,0,1:T(8,128)S(1)} %fusion.10, bf16[128,24,512]{2,0,1:T(8,128)(2,1)S(1)} %copy-done.1, s32[24]{0:T(128)S(1)} %get-tuple-element.14), kind=kOutput, calls=%fused_computation.34 | convolution fusion | flops 26214592 | bytes 6291552 | tf_op jit(solution)/shard_map/ctp,tb->cbp/dot_general | solution.py:43
  165.1 1.4 copy.76
  168.0 29.1 %reduce-scatter.5.cloned.1.call-done = bf16[128,512]{1,0:T(8,128)(2,1)} async-done(((bf16[128,4096]{1,0:T(8,128)(2,1)}), bf16[128,512]{1,0:T(8,128)(2,1)}) %reduce-scatter.5.cloned.1.call-update) | async-done | bytes 131088 | tf_op jit(solution)/shard_map/reduce_scatter | solution.py:53
  197.1 6.2 %fusion.88 = bf16[16,4,8,128]{3,2,1,0:T(8,128)(2,1)S(1)} fusion(bf16[1,16,512,512]{3,2,1,0:T(8,128)(2,1)} %param.19, bf16[16,128,512]{2,1,0:T(8,128)(2,1)S(1)} %gather_fusion.3, pred[16]{0:T(512)(128)(4,1)S(1)} %and_bitcast_fusion, bf16[128,512]{1,0:T(8,128)(2,1)} %reduce-scatter.5.cloned.1.call-done), kind=kOutput, calls=%fused_computation.56 | convolution fusion | flops 1074987008 | bytes 10747920 | tf_op jit(solution)/shard_map/cikq,ikpq->cip/dot_general | solution.py:57
  (72 shorter events, 8.5 us)
Async XLA Ops:
  7.2 115.7 %copy-start = (bf16[4,128,128]{2,1,0:T(8,128)(2,1)S(1)}, bf16[4,128,128]{2,1,0:T(8,128)(2,1)}, u32[]{:S(2)}) copy-start(bf16[4,128,128]{2,1,0:T(8,128)(2,1)} %param.21) | copy-start | bytes 393220
  7.2 38.7 %all-gather.3.cloned.1.call-start = ((), (), s32[]{:S(2)}) async-start(), calls=%async_computation.2 | async-start | bytes 2359296 | tf_op jit(solution)/shard_map/all_gather | solution.py:87
  7.9 60.4 %all-gather.5.cloned.1.call-start = ((), (), s32[]{:S(2)}) async-start(), calls=%async_computation.3 | async-start | bytes 2359296 | tf_op jit(solution)/shard_map/all_gather | solution.py:86
  9.0 13.8 %collective-permute-start = (bf16[128,512]{0,1:T(8,128)(2,1)S(1)}, bf16[128,512]{0,1:T(8,128)(2,1)S(1)}, u32[]{:S(2)}, u32[]{:S(2)}) collective-permute-start(bf16[128,512]{0,1:T(8,128)(2,1)S(1)} %copy.58), channel_id=1, source_target_pairs={{0,1},{1,4},{4,5},{5,8},{8,9},{9,12},{12,13},{13,0},{2,3},{3,6},{6... | collective-permute-start | bytes 393224 | tf_op jit(solution)/shard_map/ppermute | solution.py:17
  9.5 13.4 %collective-permute-start.1 = (bf16[128,512]{0,1:T(8,128)(2,1)S(1)}, bf16[128,512]{0,1:T(8,128)(2,1)S(1)}, u32[]{:S(2)}, u32[]{:S(2)}) collective-permute-start(bf16[128,512]{0,1:T(8,128)(2,1)S(1)} %copy.58), channel_id=1, source_target_pairs={{0,13},{1,0},{4,1},{5,4},{8,5},{9,8},{12,9},{13,12},{2,15},{3,2},{... | collective-permute-start | bytes 393224 | tf_op jit(solution)/shard_map/ppermute | solution.py:20
  13.6 103.1 %reduce-scatter.3.cloned.1.call-start = ((), (), s32[]{:S(2)}) async-start(), calls=%async_computation.4 | async-start | bytes 1179648 | tf_op jit(solution)/shard_map/reduce_scatter | solution.py:53
  22.8 7.0 %collective-permute-start.2 = (bf16[128,512]{0,1:T(8,128)(2,1)S(1)}, bf16[128,512]{0,1:T(8,128)(2,1)S(1)}, u32[]{:S(2)}, u32[]{:S(2)}) collective-permute-start(bf16[128,512]{0,1:T(8,128)(2,1)S(1)} %collective-permute-done), channel_id=1, source_target_pairs={{0,1},{1,4},{4,5},{5,8},{8,9},{9,12},{12,13},{13,0},{2,3},{3,6},{6... | collective-permute-start | bytes 393224 | tf_op jit(solution)/shard_map/ppermute | solution.py:17
  22.9 7.0 %collective-permute-start.3 = (bf16[128,512]{0,1:T(8,128)(2,1)S(1)}, bf16[128,512]{0,1:T(8,128)(2,1)S(1)}, u32[]{:S(2)}, u32[]{:S(2)}) collective-permute-start(bf16[128,512]{0,1:T(8,128)(2,1)S(1)} %collective-permute-done.1), channel_id=1, source_target_pairs={{0,13},{1,0},{4,1},{5,4},{8,5},{9,8},{12,9},{13,12},{2,15},{3,2},{... | collective-permute-start | bytes 393224 | tf_op jit(solution)/shard_map/ppermute | solution.py:20
  29.8 6.9 %collective-permute-start.4 = (bf16[128,512]{0,1:T(8,128)(2,1)S(1)}, bf16[128,512]{0,1:T(8,128)(2,1)S(1)}, u32[]{:S(2)}, u32[]{:S(2)}) collective-permute-start(bf16[128,512]{0,1:T(8,128)(2,1)S(1)} %collective-permute-done.2), channel_id=1, source_target_pairs={{0,1},{1,4},{4,5},{5,8},{8,9},{9,12},{12,13},{13,0},{2,3},{3,6},{6... | collective-permute-start | bytes 393224 | tf_op jit(solution)/shard_map/ppermute | solution.py:17
  29.9 6.8 %collective-permute-start.5 = (bf16[128,512]{0,1:T(8,128)(2,1)S(1)}, bf16[128,512]{0,1:T(8,128)(2,1)S(1)}, u32[]{:S(2)}, u32[]{:S(2)}) collective-permute-start(bf16[128,512]{0,1:T(8,128)(2,1)S(1)} %collective-permute-done.3), channel_id=1, source_target_pairs={{0,13},{1,0},{4,1},{5,4},{8,5},{9,8},{12,9},{13,12},{2,15},{3,2},{... | collective-permute-start | bytes 393224 | tf_op jit(solution)/shard_map/ppermute | solution.py:20
  36.6 6.2 %collective-permute-start.6 = (bf16[128,512]{0,1:T(8,128)(2,1)S(1)}, bf16[128,512]{0,1:T(8,128)(2,1)S(1)}, u32[]{:S(2)}, u32[]{:S(2)}) collective-permute-start(bf16[128,512]{0,1:T(8,128)(2,1)S(1)} %collective-permute-done.4), channel_id=1, source_target_pairs={{0,1},{1,4},{4,5},{5,8},{8,9},{9,12},{12,13},{13,0},{2,3},{3,6},{6... | collective-permute-start | bytes 393224 | tf_op jit(solution)/shard_map/ppermute | solution.py:17
  76.0 4.3 %copy-start.2 = (bf16[128,24,512]{2,0,1:T(8,128)(2,1)S(1)}, bf16[128,24,512]{2,0,1:T(8,128)(2,1)}, u32[]{:S(2)}) copy-start(bf16[128,24,512]{2,0,1:T(8,128)(2,1)} %get-tuple-element.18) | copy-start | bytes 9437188
  82.6 1.5 copy-start.4
  84.0 113.1 %reduce-scatter.5.cloned.1.call-start = ((), (), s32[]{:S(2)}) async-start(), calls=%async_computation.5 | async-start | bytes 1179648 | tf_op jit(solution)/shard_map/reduce_scatter | solution.py:53
  123.1 6.4 %collective-permute-start.7 = (bf16[128,512]{0,1:T(8,128)(2,1)S(1)}, bf16[128,512]{0,1:T(8,128)(2,1)S(1)}, u32[]{:S(2)}, u32[]{:S(2)}) collective-permute-start(bf16[128,512]{0,1:T(8,128)(2,1)S(1)} %bitcast.188), channel_id=1, source_target_pairs={{0,1},{1,4},{4,5},{5,8},{8,9},{9,12},{12,13},{13,0},{2,3},{3,6},{6... | collective-permute-start | bytes 393224 | tf_op jit(solution)/shard_map/ppermute | solution.py:17
  123.2 6.4 %collective-permute-start.8 = (bf16[128,512]{0,1:T(8,128)(2,1)S(1)}, bf16[128,512]{0,1:T(8,128)(2,1)S(1)}, u32[]{:S(2)}, u32[]{:S(2)}) collective-permute-start(bf16[128,512]{0,1:T(8,128)(2,1)S(1)} %bitcast.189), channel_id=1, source_target_pairs={{0,13},{1,0},{4,1},{5,4},{8,5},{9,8},{12,9},{13,12},{2,15},{3,2},{... | collective-permute-start | bytes 393224 | tf_op jit(solution)/shard_map/ppermute | solution.py:20
  129.6 6.3 %collective-permute-start.9 = (bf16[128,512]{0,1:T(8,128)(2,1)S(1)}, bf16[128,512]{0,1:T(8,128)(2,1)S(1)}, u32[]{:S(2)}, u32[]{:S(2)}) collective-permute-start(bf16[128,512]{0,1:T(8,128)(2,1)S(1)} %collective-permute-done.7), channel_id=1, source_target_pairs={{0,1},{1,4},{4,5},{5,8},{8,9},{9,12},{12,13},{13,0},{2,3},{3,6},{6... | collective-permute-start | bytes 393224 | tf_op jit(solution)/shard_map/ppermute | solution.py:17
  129.6 6.3 %collective-permute-start.10 = (bf16[128,512]{0,1:T(8,128)(2,1)S(1)}, bf16[128,512]{0,1:T(8,128)(2,1)S(1)}, u32[]{:S(2)}, u32[]{:S(2)}) collective-permute-start(bf16[128,512]{0,1:T(8,128)(2,1)S(1)} %collective-permute-done.8), channel_id=1, source_target_pairs={{0,13},{1,0},{4,1},{5,4},{8,5},{9,8},{12,9},{13,12},{2,15},{3,2},{... | collective-permute-start | bytes 393224 | tf_op jit(solution)/shard_map/ppermute | solution.py:20
  135.9 6.2 %collective-permute-start.11 = (bf16[128,512]{0,1:T(8,128)(2,1)S(1)}, bf16[128,512]{0,1:T(8,128)(2,1)S(1)}, u32[]{:S(2)}, u32[]{:S(2)}) collective-permute-start(bf16[128,512]{0,1:T(8,128)(2,1)S(1)} %collective-permute-done.9), channel_id=1, source_target_pairs={{0,1},{1,4},{4,5},{5,8},{8,9},{9,12},{12,13},{13,0},{2,3},{3,6},{6... | collective-permute-start | bytes 393224 | tf_op jit(solution)/shard_map/ppermute | solution.py:17
  135.9 6.2 %collective-permute-start.12 = (bf16[128,512]{0,1:T(8,128)(2,1)S(1)}, bf16[128,512]{0,1:T(8,128)(2,1)S(1)}, u32[]{:S(2)}, u32[]{:S(2)}) collective-permute-start(bf16[128,512]{0,1:T(8,128)(2,1)S(1)} %collective-permute-done.10), channel_id=1, source_target_pairs={{0,13},{1,0},{4,1},{5,4},{8,5},{9,8},{12,9},{13,12},{2,15},{3,2},{... | collective-permute-start | bytes 393224 | tf_op jit(solution)/shard_map/ppermute | solution.py:20
  142.1 6.2 %collective-permute-start.13 = (bf16[128,512]{0,1:T(8,128)(2,1)S(1)}, bf16[128,512]{0,1:T(8,128)(2,1)S(1)}, u32[]{:S(2)}, u32[]{:S(2)}) collective-permute-start(bf16[128,512]{0,1:T(8,128)(2,1)S(1)} %collective-permute-done.11), channel_id=1, source_target_pairs={{0,1},{1,4},{4,5},{5,8},{8,9},{9,12},{12,13},{13,0},{2,3},{3,6},{6... | collective-permute-start | bytes 393224 | tf_op jit(solution)/shard_map/ppermute | solution.py:17
  148.8 2.5 %copy-start.3 = (bf16[24,64,512]{2,1,0:T(8,128)(2,1)S(1)}, bf16[24,64,512]{2,1,0:T(8,128)(2,1)}, u32[]{:S(2)}) copy-start(bf16[24,64,512]{2,1,0:T(8,128)(2,1)} %all-gather.3.cloned.1.call-done) | copy-start | bytes 4718596
  158.6 4.3 %copy-start.1 = (bf16[128,24,512]{2,0,1:T(8,128)(2,1)S(1)}, bf16[128,24,512]{2,0,1:T(8,128)(2,1)}, u32[]{:S(2)}) copy-start(bf16[128,24,512]{2,0,1:T(8,128)(2,1)} %get-tuple-element.16) | copy-start | bytes 9437188
Sparse Core Ops, SparseCore 0:
  9.6 29.8 all-gather.2
  41.0 27.1 all-gather.4
  84.1 32.4 reduce-scatter.2
  166.7 30.3 reduce-scatter.4
